TPU v7x, 128 devices: a whole 4x4x4 slice. The times are simulated.
128 devices in a mesh: row: 8 (over x, core), col: 16 (over z, y).
Axes of the slice: x: 4, y: 4, z: 4, core: 2. Of those that a mesh axis runs over, the one named last changes fastest.
Arguments:
- amplitudes: bfloat16 [16, 16, 512, 512], P(None, 'row', 'col'), may hold values from -6 to 6
- integrals: bfloat16 [16, 512, 16, 512], P('row', 'col'), may hold values from -0.09375 to 0.09375
- occupancy: int32 [16, 16, 4, 4], replicated, may hold values from 0 to 1, as said below
Outputs:
- cycle: bfloat16 [16, 16, 512, 512], P('col', 'row')
Inputs may be any that keep to these rules, and one draw needn't show every extreme that they name: occupancy[i, k, s, t] is 1 where tile s of the first virtual index and tile t of the second are kept for the pair (i, k), else 0; it is always 1 for i = k.
All inputs are finite; a program needn't handle non-finite values.
Results may differ from a plain program's by a relative error of at most 0.001.
Values may be sent and summed in bfloat16 or wider, within the bound.
No kernel may reach another device: no remote copies, remote signals or barrier semaphores. Data moves between devices by JAX's collectives and lax.ppermute only.
A program may use at most 128 MiB of HBM per device.

v0:
```python
import jax
import jax.numpy as jnp
from jax import lax
from jax.sharding import PartitionSpec as P

DOM = 4
TILE = 128


def screen(amplitudes, occupancy):
    k_rows = amplitudes.shape[1]
    c_rows = amplitudes.shape[2]
    k_first = lax.axis_index("row") * k_rows
    c_first = lax.axis_index("col") * c_rows
    occ_rows = lax.dynamic_slice_in_dim(occupancy, k_first, k_rows, 1).astype(jnp.float32)
    c_tiles = (c_first + jnp.arange(c_rows, dtype=jnp.int32)) // TILE
    picker = (c_tiles[:, None] == jnp.arange(DOM, dtype=jnp.int32)[None, :]).astype(jnp.float32)
    tile_rows = jnp.einsum("cs,ikst->ikct", picker, occ_rows)
    mask_full = jnp.repeat(tile_rows, TILE, axis=3).astype(jnp.bfloat16)
    return amplitudes * mask_full


def per_device(amplitudes, integrals, occupancy):
    screened = screen(amplitudes, occupancy)
    regrouped = lax.all_to_all(screened, "row", split_axis=0, concat_axis=1, tiled=True)
    turned = lax.all_to_all(integrals, "col", split_axis=2, concat_axis=1, tiled=True)
    complete = lax.all_gather(turned, "row", axis=0, tiled=True)
    summed = jnp.einsum(
        "ikca,kcjb->jiba",
        lax.all_gather(regrouped, "col", axis=2, tiled=True),
        complete,
        preferred_element_type=jnp.float32,
    )
    return summed.astype(jnp.bfloat16)


def solution(mesh):
    in_specs = (P(None, "row", "col", None), P("row", "col", None, None), P())
    out_specs = P("col", "row", None, None)
    return jax.shard_map(
        per_device, mesh=mesh, in_specs=in_specs, out_specs=out_specs, check_vma=False
    )
```

profile of v0, /device:TPU:1, one launch (start us, length us, event | category | flops | bytes accessed | tf_op | source)
XLA Modules:
  0.0 225.8 jit_solution(14420888662035065762)
XLA Ops:
  6.5 0.0 copy-start
  6.5 0.0 copy-start.1
  6.5 0.0 all-gather.5.cloned.1.call-start
  6.5 1.9 copy.17
  8.4 24.4 %all_to_all.36 = bf16[2,32,16,512]{3,1,0,2:T(8,128)(2,1)S(1)} all-to-all(bf16[2,32,16,512]{3,1,0,2:T(8,128)(2,1)S(1)} %copy.17), channel_id=1, replica_groups=mesh['row'=8,'col'=16] {'col'}, dimensions={2} | all-to-all | bytes 2097152 | tf_op jit(solution)/shard_map/all_to_all | solution.py:26
  32.9 1.1 copy.18
  34.0 0.0 all-gather.5.cloned.1.call-update
  34.0 0.0 all-gather.3.cloned.1.call-start
  34.1 0.0 copy-done
  34.1 0.1 constant_dynamic-slice_fusion
  34.2 0.2 copy.23
  34.4 0.2 fusion.7
  34.6 0.3 copy.15
  34.9 1.3 broadcast_in_dim.2
  36.2 0.4 convert_element_type.29
  36.6 0.0 copy-done.1
  36.6 0.4 mul.11
  37.0 32.1 %all_to_all.37 = bf16[16,2,32,512]{3,2,1,0:T(8,128)(2,1)S(1)} all-to-all(bf16[16,2,32,512]{3,2,1,0:T(8,128)(2,1)S(1)} %mul.11), channel_id=1, replica_groups=mesh['row'=8,'col'=16] {'row'}, dimensions={0} | all-to-all | bytes 2097152 | tf_op jit(solution)/shard_map/all_to_all | solution.py:25
  69.1 1.1 copy.16
  70.1 0.0 all-gather.3.cloned.1.call-update
  70.2 23.9 %all-gather.5.cloned.1.call-done = bf16[16,512,1,512]{3,1,2,0:T(8,128)(2,1)} async-done(((bf16[2,512,1,512]{3,1,2,0:T(8,128)(2,1)}), bf16[16,512,1,512]{3,1,2,0:T(8,128)(2,1)}) %all-gather.5.cloned.1.call-update) | async-done | bytes 8388624 | tf_op jit(solution)/shard_map/all_gather | solution.py:27
  94.1 108.7 %all-gather.3.cloned.1.call-done = bf16[2,16,512,512]{3,2,1,0:T(8,128)(2,1)} async-done(((bf16[2,16,32,512]{3,2,1,0:T(8,128)(2,1)}), bf16[2,16,512,512]{3,2,1,0:T(8,128)(2,1)}) %all-gather.3.cloned.1.call-update) | async-done | bytes 16777232 | tf_op jit(solution)/shard_map/all_gather | solution.py:30
  202.8 14.8 %fusion.4 = bf16[1,2,512,512]{2,3,1,0:T(8,128)(2,1)S(1)} fusion(bf16[2,16,512,512]{3,2,1,0:T(8,128)(2,1)} %all-gather.3.cloned.1.call-done, bf16[16,512,1,512]{3,1,2,0:T(8,128)(2,1)} %all-gather.5.cloned.1.call-done), kind=kOutput, calls=%fused_computation.3 | convolution fusion | flops 8590458880 | bytes 26214400 | tf_op jit(solution)/shard_map/ikca,kcjb->jiba/dot_general | solution.py:28
  217.6 1.3 copy.20
  (1 shorter events, 0.0 us)
Async XLA Ops:
  6.5 27.5 %copy-start = (s32[16,16,4,4]{1,3,2,0:T(4,128)S(1)}, s32[16,16,4,4]{1,3,2,0:T(4,128)}, u32[]{:S(2)}) copy-start(s32[16,16,4,4]{1,3,2,0:T(4,128)} %param.5) | copy-start | bytes 49156
  6.5 30.1 %copy-start.1 = (bf16[16,2,32,512]{3,2,1,0:T(8,128)(2,1)S(1)}, bf16[16,2,32,512]{3,2,1,0:T(8,128)(2,1)}, u32[]{:S(2)}) copy-start(bf16[16,2,32,512]{3,2,1,0:T(8,128)(2,1)} %param.3) | copy-start | bytes 3145732
  6.5 87.5 %all-gather.5.cloned.1.call-start = ((), (), s32[]{:S(2)}) async-start(), calls=%async_computation.3 | async-start | bytes 9437184 | tf_op jit(solution)/shard_map/all_gather | solution.py:27
  34.0 168.8 %all-gather.3.cloned.1.call-start = ((), (), s32[]{:S(2)}) async-start(), calls=%async_computation.2 | async-start | bytes 17825792 | tf_op jit(solution)/shard_map/all_gather | solution.py:30
Sparse Core Ops, SparseCore 0:
  34.1 59.8 all-gather.4
  96.2 106.5 all-gather.2
where the time goes:
time: 226 us
  waiting for transfers between devices  133 us (59%)
  blocking collectives  56.5 us (25%)
  matrix products  15 us (7%)
  between operations  13.5 us (6%)
  local copies, waits for them, and re-layouts  7.75 us (3%)
    all_gather x1, waiting for transfers between devices, per_device(): lax.all_gather(regrouped, 'col', axis=2, tiled=True)  109 us
    all_to_all x1, blocking collectives, per_device(): lax.all_to_all(screened, 'row', split_axis=0, concat_axis=1, tiled=True)  32.1 us
    all_to_all x1, blocking collectives, per_device(): lax.all_to_all(integrals, 'col', split_axis=2, concat_axis=1, tiled=True)  24.4 us
    all_gather x1, waiting for transfers between devices, per_device(): complete = lax.all_gather(turned, 'row', axis=0, tiled=True)  23.9 us
    dot_general x1, matrix products, per_device(): jnp.einsum('ikca,kcjb->jiba', lax.all_gather(regrouped, 'col', axis=2, ti...  14.8 us
  transfers between devices with their start and end apart: 2, of which 2 were waited for; matrix products, arithmetic and copies ran while one was open for 2% of the time, Pallas kernels for 0%

commit v1 on v0

--- a/solution.py
+++ b/solution.py
@@ -24,7 +24,9 @@
     screened = screen(amplitudes, occupancy)
     regrouped = lax.all_to_all(screened, "row", split_axis=0, concat_axis=1, tiled=True)
     turned = lax.all_to_all(integrals, "col", split_axis=2, concat_axis=1, tiled=True)
-    complete = lax.all_gather(turned, "row", axis=0, tiled=True)
+    complete = jnp.concatenate(
+        lax.all_to_all(jnp.stack([turned] * lax.axis_size("row")), "row", 0, 0), axis=0
+    )
     summed = jnp.einsum(
         "ikca,kcjb->jiba",
         lax.all_gather(regrouped, "col", axis=2, tiled=True),

time: 226 us -> 190 us (0.84)
  waiting for transfers between devices: 133 us -> 0.02 us
  blocking collectives: 56.5 us -> 153 us
    all_gather x1, waiting for transfers between devices: 109 us -> 0.01 us  [per_device(): lax.all_gather(regrouped, 'col', axis=2, tiled=True)]
    all_to_all x0 -> x1, blocking collectives: none -> 103 us  [per_device(): lax.all_to_all(jnp.stack([turned] * lax.axis_size('row')), 'row', 0, 0)]
    all_gather x1 -> x0, waiting for transfers between devices: 23.9 us -> none  [per_device(): complete = lax.all_gather(turned, 'row', axis=0, tiled=True)]
    all_to_all x1, blocking collectives: 32.1 us -> 20.5 us  [per_device(): lax.all_to_all(screened, 'row', split_axis=0, concat_axis=1, tiled=True)]
    all_to_all x1, blocking collectives: 24.4 us -> 29.1 us  [per_device(): lax.all_to_all(integrals, 'col', split_axis=2, concat_axis=1, tiled=True)]
  transfers between devices with their start and end apart: 2 -> 1, of which waited for: 2 -> 0; matrix products, arithmetic and copies ran while one was open for 2% -> 1% of each run, Pallas kernels for 0% -> 0%
where the time goes in v1:
time: 190 us
  blocking collectives  153 us (81%)
  matrix products  15 us (8%)
  between operations  13.5 us (7%)
  local copies, waits for them, and re-layouts  7.04 us (4%)
    all_to_all x1, blocking collectives, per_device(): lax.all_to_all(jnp.stack([turned] * lax.axis_size('row')), 'row', 0, 0)  103 us
    all_to_all x1, blocking collectives, per_device(): lax.all_to_all(integrals, 'col', split_axis=2, concat_axis=1, tiled=True)  29.1 us
    all_to_all x1, blocking collectives, per_device(): lax.all_to_all(screened, 'row', split_axis=0, concat_axis=1, tiled=True)  20.5 us
    dot_general x1, matrix products, per_device(): jnp.einsum('ikca,kcjb->jiba', lax.all_gather(regrouped, 'col', axis=2, ti...  14.8 us
  transfers between devices with their start and end apart: 1, of which 0 were waited for; matrix products, arithmetic and copies ran while one was open for 1% of the time, Pallas kernels for 0%

profile of v1, /device:TPU:1, one launch (start us, length us, event | category | flops | bytes accessed | tf_op | source)
XLA Modules:
  0.0 189.7 jit_solution(4514563984844290594)
XLA Ops:
  6.5 0.0 copy-start
  6.5 0.0 copy-start.1
  6.5 0.0 all-gather.2.cloned.1.call-start
  6.6 0.9 copy-done
  7.4 0.1 constant_dynamic-slice_fusion
  7.6 0.2 copy.21
  7.8 0.2 fusion.1
  8.0 0.3 copy.14
  8.3 1.3 broadcast_in_dim.2
  9.5 0.4 convert_element_type.29
  10.0 1.6 mul.11
  11.6 20.5 %all_to_all.38 = bf16[16,2,32,512]{3,2,1,0:T(8,128)(2,1)S(1)} all-to-all(bf16[16,2,32,512]{3,2,1,0:T(8,128)(2,1)S(1)} %mul.11), channel_id=1, replica_groups=mesh['row'=8,'col'=16] {'row'}, dimensions={0} | all-to-all | bytes 2097152 | tf_op jit(solution)/shard_map/all_to_all | solution.py:25
  32.1 1.0 copy.15
  33.1 0.0 all-gather.2.cloned.1.call-update
  33.2 0.0 copy-done.1
  33.2 0.6 copy.16
  33.8 29.1 %all_to_all.39 = bf16[2,32,16,512]{3,1,0,2:T(8,128)(2,1)S(1)} all-to-all(bf16[2,32,16,512]{3,1,0,2:T(8,128)(2,1)S(1)} %copy.16), channel_id=1, replica_groups=mesh['row'=8,'col'=16] {'col'}, dimensions={2} | all-to-all | bytes 2097152 | tf_op jit(solution)/shard_map/all_to_all | solution.py:26
  62.9 0.1 copy.17
  63.0 0.8 stack.5
  63.8 102.9 %all_to_all.40 = bf16[8,2,512,1,512]{4,2,1,3,0:T(8,128)(2,1)} all-to-all(bf16[8,2,512,1,512]{4,2,1,3,0:T(8,128)(2,1)S(1)} %stack.5), channel_id=1, replica_groups=mesh['row'=8,'col'=16] {'row'}, dimensions={0} | all-to-all | bytes 16777216 | tf_op jit(solution)/shard_map/all_to_all | solution.py:28
  166.7 0.0 all-gather.2.cloned.1.call-done
  166.7 14.8 %fusion = bf16[1,2,512,512]{2,3,1,0:T(8,128)(2,1)S(1)} fusion(bf16[2,16,512,512]{3,2,1,0:T(8,128)(2,1)} %all-gather.2.cloned.1.call-done, bf16[16,512,512,1]{2,1,0,3:T(8,128)(2,1)} %bitcast.32), kind=kOutput, calls=%fused_computation.1 | convolution fusion | flops 8590458880 | bytes 26214400 | tf_op jit(solution)/shard_map/ikca,kcjb->jiba/dot_general | solution.py:30
  181.5 1.3 copy.18
  (1 shorter events, 0.0 us)
Async XLA Ops:
  6.5 0.9 copy-start
  6.5 26.6 %copy-start.1 = (bf16[2,32,16,512]{3,2,1,0:T(8,128)(2,1)S(1)}, bf16[2,32,16,512]{3,2,1,0:T(8,128)(2,1)}, u32[]{:S(2)}) copy-start(bf16[2,32,16,512]{3,2,1,0:T(8,128)(2,1)} %param.4) | copy-start | bytes 3145732
  6.5 160.2 %all-gather.2.cloned.1.call-start = ((), (), s32[]{:S(2)}) async-start(), calls=%async_computation.3 | async-start | bytes 17825792 | tf_op jit(solution)/shard_map/all_gather | solution.py:32
Sparse Core Ops, SparseCore 0:
  33.3 117.0 all-gather.1
